TPU v7x, 256 devices: a whole 4x4x8 slice. The times are simulated.
256 devices in a mesh: dp: 16 (over z_hi, x, core), fsdp: 16 (over y, z_lo).
Axes of the slice: x: 4, y: 4, z: 8 (z_hi: 2, z_lo: 4; z = z_hi * 4 + z_lo), core: 2. Of those that a mesh axis runs over, the one named last changes fastest.
Arguments:
- token_ids: int32 [32768], P('dp'), may hold values from 0 to 30527, as said below
- embed_table: bfloat16 [30528, 768], P('fsdp'), may hold values from -16 to 16, as said below
- w_qkv: bfloat16 [768, 2304], P('fsdp'), may hold values from -2 to 2
- w_out: bfloat16 [768, 768], P('fsdp'), may hold values from -0.21875 to 0.21875
- ln_gain: float32 [768], replicated, may hold values from 0.5 to 1.5
- ln_bias: float32 [768], replicated, may hold values from -1 to 1
- centroids_t: bfloat16 [768, 32768], P('fsdp', 'dp'), may hold values from -24 to 24
- assignments: int32 [32768], replicated, may hold values from 0 to 32767, as said below
Outputs:
- token_loss: float32 [32768], P(('dp', 'fsdp'))
- new_centroids: float32 [32768, 768], P(('dp', 'fsdp'))
Inputs may be any that keep to these rules, and one draw needn't show every extreme that they name: `token_ids`: id 0 is padding; a passage may end in a run of padding. `embed_table`: token embeddings of order one. `assignments`: cluster sizes are skewed.
All inputs are finite; a program needn't handle non-finite values.
Results may differ from a plain program's by a relative error of at most 0.0055.
Values may be sent and summed in bfloat16 or wider, within the bound.
No kernel may reach another device: no remote copies, remote signals or barrier semaphores. Data moves between devices by JAX's collectives and lax.ppermute only.
A program may use at most 64 MiB of HBM per device.

v0:
```python
import math
import jax
import jax.numpy as jnp
from jax import lax
from jax.sharding import Mesh
from jax.sharding import PartitionSpec as P

HEADS = 12
HEAD = 64
SEQ = 128
FSDP = ("fsdp_0", "fsdp_1")
DP_FSDP = ("dp", "fsdp_0", "fsdp_1")


def in_blocks(shard, dim, devices):
    before, after = (shard.shape[:dim], shard.shape[dim + 1 :])
    return jnp.moveaxis(shard.reshape(*before, devices, -1, *after), dim, 0)


def sent_and_summed(shard, axis, dim):
    devices = lax.axis_size(axis)
    parts = lax.all_to_all(in_blocks(shard, dim, devices), axis, 0, 0, tiled=True)
    return jnp.sum(parts.astype(jnp.float32), axis=0)


def in_one_piece(arrays, axis, dim, along):
    both = jnp.concatenate(arrays, axis=along)
    filled, at, done = (lax.all_gather(both, axis, axis=dim, tiled=True), 0, [])
    for a in arrays:
        done.append(lax.slice_in_dim(filled, at, at + a.shape[along], axis=along))
        at += a.shape[along]
    return tuple(done)


def sent_together(arrays, axis, split_dim, concat_dim, along):
    widths = [a.shape[along] for a in arrays]
    both = jnp.concatenate(arrays, axis=along)
    filled = lax.all_to_all(both, axis, split_axis=split_dim, concat_axis=concat_dim, tiled=True)
    return tuple(jnp.split(filled, [sum(widths[:k]) for k in range(1, len(widths))], axis=along))


def scatter_axes(shard, axes, dim):
    if not axes:
        return shard
    nearer = lax.psum_scatter(shard, axes[0], scatter_dimension=dim, tiled=True)
    return scatter_axes(nearer, axes[1:], dim)


def layer_norm(values, ln_gain, ln_bias):
    center = values - jnp.mean(values, axis=-1, keepdims=True)
    spread = jnp.mean(center * center, axis=-1, keepdims=True)
    return center * lax.rsqrt(spread + 1e-05) * ln_gain + ln_bias


def encode(inputs, qkv_full, out_full, ln_gain, ln_bias):
    passages = inputs.shape[0] // SEQ
    packed = jnp.dot(inputs, qkv_full, preferred_element_type=jnp.float32).astype(jnp.bfloat16)
    packed = packed.reshape(passages, SEQ, 3, HEADS, HEAD)
    scores = jnp.einsum(
        "bqhd,bkhd->bhqk", packed[:, :, 0], packed[:, :, 1], preferred_element_type=jnp.float32
    ) * (1.0 / math.sqrt(HEAD))
    probs = jax.nn.softmax(scores, axis=-1).astype(jnp.bfloat16)
    context = jnp.einsum(
        "bhqk,bkhd->bqhd", probs, packed[:, :, 2], preferred_element_type=jnp.float32
    )
    context = context.astype(jnp.bfloat16).reshape(inputs.shape[0], HEADS * HEAD)
    mixed = jnp.dot(context, out_full, preferred_element_type=jnp.float32) + inputs.astype(
        jnp.float32
    )
    return layer_norm(mixed, ln_gain, ln_bias).astype(jnp.bfloat16)


def shards(token_ids, embed_table, w_qkv, w_out, ln_gain, ln_bias, centroids_t, assignments):
    dp_size = lax.axis_size("dp")
    fsdp_size = lax.axis_size(FSDP)
    dp_rank = lax.axis_index("dp")
    fsdp_rank = lax.axis_index(FSDP)
    vocab_rows = embed_table.shape[0]
    local_ids = token_ids - fsdp_rank * vocab_rows
    inside = (local_ids >= 0) & (local_ids < vocab_rows)
    looked = jnp.take(embed_table, jnp.clip(local_ids, 0, vocab_rows - 1), axis=0)
    looked = jnp.where(inside[:, None], looked, jnp.zeros_like(looked))
    inputs = sent_and_summed(looked, FSDP, 0).astype(jnp.bfloat16)
    qkv_full, out_full, cent_full = in_one_piece((w_qkv, w_out, centroids_t), FSDP, 0, 1)
    encoded = encode(inputs, qkv_full, out_full, ln_gain, ln_bias)
    own_rows = encoded.shape[0]
    width = encoded.shape[1]
    block_width = cent_full.shape[1]
    per_dev = block_width // fsdp_size
    slab = lax.all_gather(encoded, "dp", axis=0, tiled=True)
    slab_assign = lax.dynamic_index_in_dim(
        assignments.reshape(dp_size, fsdp_size, own_rows), fsdp_rank, 1, keepdims=False
    ).reshape(-1)
    owned = slab_assign - dp_rank * block_width
    slab_rows = slab.shape[0]
    step_rows = math.gcd(slab_rows, 512)
    columns = jnp.arange(block_width, dtype=jnp.int32)

    def visit(totals, pieces):
        block_rows, local = pieces
        logits = jnp.dot(block_rows, cent_full, preferred_element_type=jnp.float32)
        peak = jnp.max(logits, axis=1)
        mass = jnp.sum(jnp.exp(logits - peak[:, None]), axis=1)
        hits = local[:, None] == columns[None, :]
        picked = jnp.sum(jnp.where(hits, logits, 0.0), axis=1)
        totals = totals + lax.dot_general(
            hits.astype(jnp.bfloat16),
            block_rows,
            (((0,), (0,)), ((), ())),
            preferred_element_type=jnp.float32,
        )
        return (totals, (peak, mass, picked))

    start = jnp.zeros((block_width, width), jnp.float32)
    partial_value, stats = lax.scan(
        visit,
        start,
        (
            slab.reshape(slab_rows // step_rows, step_rows, width),
            owned.reshape(slab_rows // step_rows, step_rows),
        ),
    )
    peaks, masses, picks = (stats[0].reshape(-1), stats[1].reshape(-1), stats[2].reshape(-1))
    got_peaks, got_masses, got_picks = sent_together(
        (
            peaks.reshape(dp_size, own_rows),
            masses.reshape(dp_size, own_rows),
            picks.reshape(dp_size, own_rows),
        ),
        "dp",
        0,
        0,
        1,
    )
    peak_own = jnp.max(got_peaks, axis=0)
    mass_own = jnp.sum(got_masses * jnp.exp(got_peaks - peak_own[None, :]), axis=0)
    pick_own = jnp.sum(got_picks, axis=0)
    token_loss = jnp.log(mass_own) + peak_own - pick_own
    totals = scatter_axes(partial_value, FSDP, 0)
    base = dp_rank * block_width + fsdp_rank * per_dev
    targets = base + jnp.arange(per_dev, dtype=jnp.int32)
    counts = jnp.sum((assignments[:, None] == targets[None, :]).astype(jnp.int32), axis=0)
    previous = lax.dynamic_slice_in_dim(cent_full, fsdp_rank * per_dev, per_dev, 1).T.astype(
        jnp.float32
    )
    new_centroids = jnp.where(
        counts[:, None] > 0, totals / jnp.maximum(counts, 1)[:, None].astype(jnp.float32), previous
    )
    return (token_loss, new_centroids)


def solution(mesh):
    finer = Mesh(mesh.devices.reshape(mesh.shape["dp"], 4, 4), ("dp", "fsdp_0", "fsdp_1"))
    placed = (P("dp"), P(FSDP, None), P(FSDP, None), P(FSDP, None), P(), P(), P(FSDP, "dp"), P())
    return jax.shard_map(
        shards,
        mesh=finer,
        in_specs=placed,
        out_specs=(P(DP_FSDP), P(DP_FSDP, None)),
        check_vma=False,
    )
```

profile of v0, /device:TPU:1, one launch (start us, length us, event | category | flops | bytes accessed | tf_op | source)
XLA Modules:
  0.0 507.1 jit_solution(12758839840471704334)
XLA Ops:
  7.2 2.1 pad_maximum_fusion
  9.4 0.7 fusion.19
  10.1 9.5 %gather_fusion = bf16[2048,768]{1,0:T(8,128)(2,1)} fusion(bf16[1908,768]{1,0:T(8,128)(2,1)S(1)} %copy-done, s32[2048]{0:T(1024)S(1)} %fusion.19), kind=kCustom, calls=%fused_computation | custom fusion | bytes 6299648 | tf_op jit(solution)/shard_map/jit(_take)/gather | solution.py:81
  19.6 2.3 select_select_fusion
  21.8 157.9 %all_to_all.17 = bf16[16,128,768]{2,1,0:T(8,128)(2,1)} all-to-all(bf16[16,128,768]{2,1,0:T(8,128)(2,1)S(1)} %select_select_fusion), channel_id=1, replica_groups=mesh['dp'=16,'fsdp_0'=4,'fsdp_1'=4] {'fsdp_0','fsdp_1'}, dimensions={0} | all-to-all | bytes 6291456 | tf_op jit(solution)/shard_map/all_to_all | solution.py:22
  179.7 2.3 reduce_sum.84
  182.1 69.7 %all-gather.3.cloned.1.call-done = bf16[768,5120]{1,0:T(8,128)(2,1)} async-done(((bf16[48,5120]{1,0:T(8,128)(2,1)}), bf16[768,5120]{1,0:T(8,128)(2,1)}) %all-gather.3.cloned.1.call-update) | async-done | bytes 7864336 | tf_op jit(solution)/shard_map/all_gather | solution.py:28
  251.8 3.5 convolution_convert_fusion
  255.3 1.4 copy.28
  256.7 1.3 convolution_multiply_fusion
  258.0 0.4 fusion.23
  258.4 2.5 convolution_convert_fusion.1
  260.9 1.8 fusion.24
  262.7 0.2 multiply_reduce_fusion
  263.0 0.8 add_convert_fusion
  263.9 0.9 subtract_reduce_fusion
  264.8 3.9 slice.31
  268.7 66.8 %all-gather.5.cloned.1.call-done = bf16[2048,768]{1,0:T(8,128)(2,1)} async-done(((bf16[128,768]{1,0:T(8,128)(2,1)}), bf16[2048,768]{1,0:T(8,128)(2,1)}) %all-gather.5.cloned.1.call-update) | async-done | bytes 3145744 | tf_op jit(solution)/shard_map/all_gather | solution.py:90
  335.5 51.3 %while.17 = (s32[]{:T(128)}, f32[2048,768]{1,0:T(8,128)}, f32[4,512]{1,0:T(4,128)S(1)}, f32[4,512]{1,0:T(4,128)S(1)}, f32[4,512]{1,0:T(4,128)S(1)}, /*index=5*/s...) while((s32[]{:T(128)}, f32[2048,768]{1,0:T(8,128)}, ...), condition=%wide.region_9.10_spmd.clone, body=%wide.region_5.9_spmd.clone.sunk | while | flops 3231709696 | bytes 25719936 | solution.py:115
  335.5 4.0 fusion.35
  339.5 1.4 fusion.36
  340.9 0.1 dynamic_update_slice.17
  341.0 0.1 dynamic_update_slice.18
  341.0 5.8 %select_add_fusion.2 = f32[2048,768]{1,0:T(8,128)} fusion(f32[2048,768]{1,0:T(8,128)} %get-tuple-element.199, pred[]{:T(512)S(6)} %compare.3, s32[512]{0:T(512)S(1)} %bitcast.70, bf16[4,512,768]{2,1,0:T(8,128)(2,1)} %get-tuple-element.214, s32[]{:T(128)} %get-tuple-element.198), kind=kOutput, calls=%fused_computation.2.clone.1 | convolution fusion | flops 1614807040 | bytes 13371905 | tf_op jit(solution)/shard_map/while/body/eval_jaxpr/dot_general | solution.py:106
  346.9 4.0 fusion.35
  350.9 1.4 fusion.36
  352.3 0.1 dynamic_update_slice.17
  352.4 0.1 dynamic_update_slice.18
  352.4 7.7 %select_add_fusion.2 = f32[2048,768]{1,0:T(8,128)} fusion(f32[2048,768]{1,0:T(8,128)} %get-tuple-element.199, pred[]{:T(512)S(6)} %compare.3, s32[512]{0:T(512)S(1)} %bitcast.70, bf16[4,512,768]{2,1,0:T(8,128)(2,1)} %get-tuple-element.214, s32[]{:T(128)} %get-tuple-element.198), kind=kOutput, calls=%fused_computation.2.clone.1 | convolution fusion | flops 1614807040 | bytes 13371905 | tf_op jit(solution)/shard_map/while/body/eval_jaxpr/dot_general | solution.py:106
  360.2 4.0 fusion.35
  364.2 1.4 fusion.36
  365.6 0.1 dynamic_update_slice.17
  365.7 0.1 dynamic_update_slice.18
  365.7 7.7 %select_add_fusion.2 = f32[2048,768]{1,0:T(8,128)} fusion(f32[2048,768]{1,0:T(8,128)} %get-tuple-element.199, pred[]{:T(512)S(6)} %compare.3, s32[512]{0:T(512)S(1)} %bitcast.70, bf16[4,512,768]{2,1,0:T(8,128)(2,1)} %get-tuple-element.214, s32[]{:T(128)} %get-tuple-element.198), kind=kOutput, calls=%fused_computation.2.clone.1 | convolution fusion | flops 1614807040 | bytes 13371905 | tf_op jit(solution)/shard_map/while/body/eval_jaxpr/dot_general | solution.py:106
  373.5 4.0 fusion.35
  377.5 1.4 fusion.36
  378.9 0.1 dynamic_update_slice.17
  379.0 7.7 %select_add_fusion.2 = f32[2048,768]{1,0:T(8,128)} fusion(f32[2048,768]{1,0:T(8,128)} %get-tuple-element.199, pred[]{:T(512)S(6)} %compare.3, s32[512]{0:T(512)S(1)} %bitcast.70, bf16[4,512,768]{2,1,0:T(8,128)(2,1)} %get-tuple-element.214, s32[]{:T(128)} %get-tuple-element.198), kind=kOutput, calls=%fused_computation.2.clone.1 | convolution fusion | flops 1614807040 | bytes 13371905 | tf_op jit(solution)/shard_map/while/body/eval_jaxpr/dot_general | solution.py:106
  386.8 6.6 %copy.30 = f32[2048,768]{0,1:T(8,128)} copy(f32[2048,768]{1,0:T(8,128)} %get-tuple-element.55) | data formatting | bytes 12582912 | tf_op jit(solution)/shard_map/while | solution.py:115
  393.5 62.0 %reduce-scatter.3.cloned.1.call-done = f32[512,768]{0,1:T(8,128)} async-done(((f32[2048,768]{0,1:T(8,128)}), f32[512,768]{0,1:T(8,128)}) %reduce-scatter.3.cloned.1.call-update) | async-done | bytes 1572880 | tf_op jit(solution)/shard_map/reduce_scatter | solution.py:45
  455.5 5.6 %convert_reduce_fusion = s32[128]{0:T(128)S(1)} fusion(s32[128]{0:T(128)S(1)} %iota_add_fusion, s32[32768]{0:T(1024)S(1)} %copy-done.2), kind=kLoop, calls=%fused_computation.18 | loop fusion | flops 12582784 | bytes 132096 | tf_op jit(solution)/shard_map/reduce_sum | solution.py:142
  461.2 0.6 all_to_all.12
  461.8 10.1 %all-to-all-start.1 = ((f32[16,1,384]{2,1,0:T(1,128)}), f32[16,1,384]{2,1,0:T(1,128)S(1)}, u32[]{:S(2)}, u32[]{:S(2)}) async-start(f32[16,1,384]{2,1,0:T(1,128)} %all_to_all.12), calls=%async_computation.1 | async-start | bytes 49152 | tf_op jit(solution)/shard_map/all_to_all | solution.py:38
  471.9 9.7 %all-to-all-done.1 = f32[16,1,384]{2,1,0:T(1,128)S(1)} async-done(((f32[16,1,384]{2,1,0:T(1,128)}), f32[16,1,384]{2,1,0:T(1,128)S(1)}, u32[]{:S(2)}, u32[]{:S(2)}) %all-to-all-start.1) | async-done | bytes 24608 | tf_op jit(solution)/shard_map/all_to_all | solution.py:38
  481.7 0.5 add_subtract_fusion
  482.2 16.4 %reduce-scatter.5.cloned.1.call-done = f32[128,768]{0,1:T(8,128)} async-done(((f32[512,768]{0,1:T(8,128)}), f32[128,768]{0,1:T(8,128)}) %reduce-scatter.5.cloned.1.call-update) | async-done | bytes 393232 | tf_op jit(solution)/shard_map/reduce_scatter | solution.py:45
  498.6 1.1 bitcast_select_fusion
  499.6 0.9 copy.31
  (47 shorter events, 0.6 us)
Async XLA Ops:
  7.2 2.9 copy-start
  7.2 244.6 %all-gather.3.cloned.1.call-start = ((), (), s32[]{:S(2)}) async-start(), calls=%async_computation.4 | async-start | bytes 8355840 | tf_op jit(solution)/shard_map/all_gather | solution.py:28
  9.3 326.2 %all-gather.5.cloned.1.call-start = ((), (), s32[]{:S(2)}) async-start(), calls=%async_computation.5 | async-start | bytes 3342336 | tf_op jit(solution)/shard_map/all_gather | solution.py:90
  10.1 9.5 %copy-start.3 = (s32[2048]{0:T(1024)S(1)}, s32[2048]{0:T(1024)}, u32[]{:S(2)}) copy-start(s32[2048]{0:T(1024)} %param.10) | copy-start | bytes 24580
  182.1 69.7 %copy-start.1 = (bf16[128,768]{1,0:T(8,128)(2,1)}, bf16[128,768]{1,0:T(8,128)(2,1)S(1)}, u32[]{:S(2)}) copy-start(bf16[128,768]{1,0:T(8,128)(2,1)S(1)} %reduce_sum.84) | copy-start | bytes 589828
  256.7 6.3 %copy-start.4 = (f32[768]{0:T(1024)S(1)}, f32[768]{0:T(1024)}, u32[]{:S(2)}) copy-start(f32[768]{0:T(1024)} %param.15) | copy-start | bytes 9220
  256.7 6.3 %copy-start.5 = (f32[768]{0:T(1024)S(1)}, f32[768]{0:T(1024)}, u32[]{:S(2)}) copy-start(f32[768]{0:T(1024)} %param.14) | copy-start | bytes 9220
  263.8 191.7 %reduce-scatter.3.cloned.1.call-start = ((), (), s32[]{:S(2)}) async-start(), calls=%async_computation.6 | async-start | bytes 7864320 | tf_op jit(solution)/shard_map/reduce_scatter | solution.py:45
  393.4 62.1 %copy-start.2 = (s32[32768]{0:T(1024)S(1)}, s32[32768]{0:T(1024)}, u32[]{:S(2)}) copy-start(s32[32768]{0:T(1024)} %param.17) | copy-start | bytes 393220
  393.4 105.2 %reduce-scatter.5.cloned.1.call-start = ((), (), s32[]{:S(2)}) async-start(), calls=%async_computation.7 | async-start | bytes 1966080 | tf_op jit(solution)/shard_map/reduce_scatter | solution.py:45
  461.8 19.8 %all-to-all-start.1 = ((f32[16,1,384]{2,1,0:T(1,128)}), f32[16,1,384]{2,1,0:T(1,128)S(1)}, u32[]{:S(2)}, u32[]{:S(2)}) async-start(f32[16,1,384]{2,1,0:T(1,128)} %all_to_all.12), calls=%async_computation.1 | async-start | bytes 49152 | tf_op jit(solution)/shard_map/all_to_all | solution.py:38
Sparse Core Ops, SparseCore 0:
  9.8 241.9 all-gather.2
  263.9 71.5 all-gather.4
  393.5 61.9 reduce-scatter.2
  457.9 40.6 reduce-scatter.4
where the time goes:
time: 508 us; the launch traced here: 507 us
  waiting for transfers between devices  225 us (44%)
  blocking collectives  158 us (31%)
  matrix products  54.5 us (11%)
  local copies, waits for them, and re-layouts  23.6 us (5%)
  other arithmetic  22.2 us (4%)
  between operations  14 us (3%)
  starting transfers between devices  10.2 us (2%)
    all_to_all x1, blocking collectives, sent_and_summed(): lax.all_to_all(in_blocks(shard, dim, devices), axis, 0, 0, tiled=True)  158 us
    reduce_scatter x2, waiting for transfers between devices, scatter_axes(): nearer = lax.psum_scatter(shard, axes[0], scatter_dimension=dim, tiled=True)  78.4 us
    all_gather x1, waiting for transfers between devices, in_one_piece(): filled, at, done = (lax.all_gather(both, axis, axis=dim, tiled=True), 0, [])  69.7 us
    all_gather x1, waiting for transfers between devices, shards(): slab = lax.all_gather(encoded, 'dp', axis=0, tiled=True)  66.8 us
    dot_general x4, matrix products, visit(): lax.dot_general(hits.astype(jnp.bfloat16), block_rows, (((0,), (0,)), (()...  28.8 us
    dot_general x4, matrix products, visit(): logits = jnp.dot(block_rows, cent_full, preferred_element_type=jnp.float32)  16.1 us
  transfers between devices with their start and end apart: 5, of which 5 were waited for; matrix products, arithmetic and copies ran while one was open for 5% of the time, Pallas kernels for 0%

commit v1 on v0

--- a/solution.py
+++ b/solution.py
@@ -10,6 +10,13 @@
 SEQ = 128
 FSDP = ("fsdp_0", "fsdp_1")
 DP_FSDP = ("dp", "fsdp_0", "fsdp_1")
+
+
+def exchange_gather(shard, name, along):
+    devices = lax.axis_size(name)
+    blocks = jnp.stack([shard for _ in range(devices)])
+    blocks = lax.all_to_all(blocks, name, split_axis=0, concat_axis=0)
+    return jnp.concatenate(blocks, axis=along)
 
 
 def in_blocks(shard, dim, devices):
@@ -87,7 +94,7 @@
     width = encoded.shape[1]
     block_width = cent_full.shape[1]
     per_dev = block_width // fsdp_size
-    slab = lax.all_gather(encoded, "dp", axis=0, tiled=True)
+    slab = exchange_gather(encoded, "dp", 0)
     slab_assign = lax.dynamic_index_in_dim(
         assignments.reshape(dp_size, fsdp_size, own_rows), fsdp_rank, 1, keepdims=False
     ).reshape(-1)

time: 508 us -> 531 us (1.045)
  waiting for transfers between devices: 225 us -> 238 us
  starting transfers between devices: 10.2 us -> 20 us
    all_gather x1 -> x0, waiting for transfers between devices: 66.8 us -> none  [shards(): slab = lax.all_gather(encoded, 'dp', axis=0, tiled=True)]
    reduce_scatter x2, waiting for transfers between devices: 78.4 us -> 121 us  [scatter_axes(): nearer = lax.psum_scatter(shard, axes[0], scatter_dimension=dim, tiled=True)]
    all_to_all x0 -> x1, waiting for transfers between devices: none -> 38.3 us  [exchange_gather(): blocks = lax.all_to_all(blocks, name, split_axis=0, concat_axis=0)]
    all_to_all x0 -> x1, starting transfers between devices: none -> 9.83 us  [exchange_gather(): blocks = lax.all_to_all(blocks, name, split_axis=0, concat_axis=0)]
where the time goes in v1:
time: 531 us; the launch traced here: 530 us
  waiting for transfers between devices  238 us (45%)
  blocking collectives  158 us (30%)
  matrix products  54.5 us (10%)
  local copies, waits for them, and re-layouts  25.6 us (5%)
  other arithmetic  20.7 us (4%)
  starting transfers between devices  20 us (4%)
  between operations  14 us (3%)
    all_to_all x1, blocking collectives, sent_and_summed(): lax.all_to_all(in_blocks(shard, dim, devices), axis, 0, 0, tiled=True)  158 us
    reduce_scatter x2, waiting for transfers between devices, scatter_axes(): nearer = lax.psum_scatter(shard, axes[0], scatter_dimension=dim, tiled=True)  121 us
    all_gather x1, waiting for transfers between devices, in_one_piece(): filled, at, done = (lax.all_gather(both, axis, axis=dim, tiled=True), 0, [])  69.1 us
    all_to_all x1, waiting for transfers between devices, exchange_gather(): blocks = lax.all_to_all(blocks, name, split_axis=0, concat_axis=0)  38.3 us
    dot_general x4, matrix products, visit(): lax.dot_general(hits.astype(jnp.bfloat16), block_rows, (((0,), (0,)), (()...  28.8 us
    dot_general x4, matrix products, visit(): logits = jnp.dot(block_rows, cent_full, preferred_element_type=jnp.float32)  16.1 us
  transfers between devices with their start and end apart: 5, of which 5 were waited for; matrix products, arithmetic and copies ran while one was open for 5% of the time, Pallas kernels for 0%

profile of v1, /device:TPU:1, one launch (start us, length us, event | category | flops | bytes accessed | tf_op | source)
XLA Modules:
  0.0 530.4 jit_solution(1938286921218316801)
XLA Ops:
  7.2 2.1 pad_maximum_fusion
  9.3 0.7 fusion.19
  10.0 9.5 %gather_fusion = bf16[2048,768]{1,0:T(8,128)(2,1)} fusion(bf16[1908,768]{1,0:T(8,128)(2,1)S(1)} %copy-done, s32[2048]{0:T(1024)S(1)} %fusion.19), kind=kCustom, calls=%fused_computation | custom fusion | bytes 6299648 | tf_op jit(solution)/shard_map/jit(_take)/gather | solution.py:88
  19.5 2.3 select_select_fusion
  21.8 157.9 %all_to_all.22 = bf16[16,128,768]{2,1,0:T(8,128)(2,1)} all-to-all(bf16[16,128,768]{2,1,0:T(8,128)(2,1)S(1)} %select_select_fusion), channel_id=1, replica_groups=mesh['dp'=16,'fsdp_0'=4,'fsdp_1'=4] {'fsdp_0','fsdp_1'}, dimensions={0} | all-to-all | bytes 6291456 | tf_op jit(solution)/shard_map/all_to_all | solution.py:29
  179.7 2.3 reduce_sum.84
  182.0 69.1 %all-gather.2.cloned.1.call-done = bf16[768,5120]{1,0:T(8,128)(2,1)} async-done(((bf16[48,5120]{1,0:T(8,128)(2,1)}), bf16[768,5120]{1,0:T(8,128)(2,1)}) %all-gather.2.cloned.1.call-update) | async-done | bytes 7864336 | tf_op jit(solution)/shard_map/all_gather | solution.py:35
  251.1 3.5 convolution_convert_fusion
  254.6 1.4 copy.28
  256.0 1.3 convolution_multiply_fusion
  257.3 0.4 fusion.23
  257.7 2.5 convolution_convert_fusion.1
  260.3 1.8 fusion.24
  262.1 0.2 multiply_reduce_fusion
  262.3 0.1 add_convert_fusion
  262.4 2.0 stack.2
  264.4 9.8 %all-to-all-start.1 = ((bf16[16,128,768]{2,1,0:T(8,128)(2,1)}), bf16[16,128,768]{2,1,0:T(8,128)(2,1)}, u32[]{:S(2)}, u32[]{:S(2)}) async-start(bf16[16,128,768]{2,1,0:T(8,128)(2,1)} %stack.2), calls=%async_computation.1 | async-start | bytes 6291456 | tf_op jit(solution)/shard_map/all_to_all | solution.py:18
  274.4 3.9 slice.31
  278.3 38.3 %all-to-all-done.1 = bf16[16,128,768]{2,1,0:T(8,128)(2,1)} async-done(((bf16[16,128,768]{2,1,0:T(8,128)(2,1)}), bf16[16,128,768]{2,1,0:T(8,128)(2,1)}, u32[]{:S(2)}, u32[]{:S(2)}) %all-to-all-start.1) | async-done | bytes 3145760 | tf_op jit(solution)/shard_map/all_to_all | solution.py:18
  316.7 51.3 %while.17 = (s32[]{:T(128)}, f32[2048,768]{1,0:T(8,128)}, f32[4,512]{1,0:T(4,128)S(1)}, f32[4,512]{1,0:T(4,128)S(1)}, f32[4,512]{1,0:T(4,128)S(1)}, /*index=5*/s...) while((s32[]{:T(128)}, f32[2048,768]{1,0:T(8,128)}, ...), condition=%wide.region_9.10_spmd.clone, body=%wide.region_5.9_spmd.clone.sunk | while | flops 3231709696 | bytes 25719936 | solution.py:122
  316.7 4.0 fusion.35
  320.7 1.4 fusion.36
  322.1 0.1 dynamic_update_slice.17
  322.2 0.1 dynamic_update_slice.18
  322.2 5.8 %select_add_fusion.2 = f32[2048,768]{1,0:T(8,128)} fusion(f32[2048,768]{1,0:T(8,128)} %get-tuple-element.199, pred[]{:T(512)S(6)} %compare.3, s32[512]{0:T(512)S(1)} %bitcast.69, bf16[4,512,768]{2,1,0:T(8,128)(2,1)} %get-tuple-element.214, s32[]{:T(128)} %get-tuple-element.198), kind=kOutput, calls=%fused_computation.2.clone.1 | convolution fusion | flops 1614807040 | bytes 13371905 | tf_op jit(solution)/shard_map/while/body/eval_jaxpr/dot_general | solution.py:113
  328.1 4.0 fusion.35
  332.1 1.4 fusion.36
  333.5 0.1 dynamic_update_slice.17
  333.6 0.1 dynamic_update_slice.18
  333.6 7.7 %select_add_fusion.2 = f32[2048,768]{1,0:T(8,128)} fusion(f32[2048,768]{1,0:T(8,128)} %get-tuple-element.199, pred[]{:T(512)S(6)} %compare.3, s32[512]{0:T(512)S(1)} %bitcast.69, bf16[4,512,768]{2,1,0:T(8,128)(2,1)} %get-tuple-element.214, s32[]{:T(128)} %get-tuple-element.198), kind=kOutput, calls=%fused_computation.2.clone.1 | convolution fusion | flops 1614807040 | bytes 13371905 | tf_op jit(solution)/shard_map/while/body/eval_jaxpr/dot_general | solution.py:113
  341.3 4.0 fusion.35
  345.4 1.4 fusion.36
  346.8 0.1 dynamic_update_slice.17
  346.9 0.1 dynamic_update_slice.18
  346.9 7.7 %select_add_fusion.2 = f32[2048,768]{1,0:T(8,128)} fusion(f32[2048,768]{1,0:T(8,128)} %get-tuple-element.199, pred[]{:T(512)S(6)} %compare.3, s32[512]{0:T(512)S(1)} %bitcast.69, bf16[4,512,768]{2,1,0:T(8,128)(2,1)} %get-tuple-element.214, s32[]{:T(128)} %get-tuple-element.198), kind=kOutput, calls=%fused_computation.2.clone.1 | convolution fusion | flops 1614807040 | bytes 13371905 | tf_op jit(solution)/shard_map/while/body/eval_jaxpr/dot_general | solution.py:113
  354.7 4.0 fusion.35
  358.7 1.4 fusion.36
  360.2 7.7 %select_add_fusion.2 = f32[2048,768]{1,0:T(8,128)} fusion(f32[2048,768]{1,0:T(8,128)} %get-tuple-element.199, pred[]{:T(512)S(6)} %compare.3, s32[512]{0:T(512)S(1)} %bitcast.69, bf16[4,512,768]{2,1,0:T(8,128)(2,1)} %get-tuple-element.214, s32[]{:T(128)} %get-tuple-element.198), kind=kOutput, calls=%fused_computation.2.clone.1 | convolution fusion | flops 1614807040 | bytes 13371905 | tf_op jit(solution)/shard_map/while/body/eval_jaxpr/dot_general | solution.py:113
  367.9 6.6 %copy.30 = f32[2048,768]{0,1:T(8,128)} copy(f32[2048,768]{1,0:T(8,128)} %get-tuple-element.55) | data formatting | bytes 12582912 | tf_op jit(solution)/shard_map/while | solution.py:122
  374.6 104.0 %reduce-scatter.3.cloned.1.call-done = f32[512,768]{0,1:T(8,128)} async-done(((f32[2048,768]{0,1:T(8,128)}), f32[512,768]{0,1:T(8,128)}) %reduce-scatter.3.cloned.1.call-update) | async-done | bytes 1572880 | tf_op jit(solution)/shard_map/reduce_scatter | solution.py:52
  478.6 5.6 %convert_reduce_fusion = s32[128]{0:T(128)S(1)} fusion(s32[128]{0:T(128)S(1)} %iota_add_fusion, s32[32768]{0:T(1024)S(1)} %copy-done.2), kind=kLoop, calls=%fused_computation.18 | loop fusion | flops 12582784 | bytes 132096 | tf_op jit(solution)/shard_map/reduce_sum | solution.py:149
  484.3 0.6 all_to_all.16
  485.0 10.1 %all-to-all-start.2 = ((f32[16,1,384]{2,1,0:T(1,128)}), f32[16,1,384]{2,1,0:T(1,128)S(1)}, u32[]{:S(2)}, u32[]{:S(2)}) async-start(f32[16,1,384]{2,1,0:T(1,128)} %all_to_all.16), calls=%async_computation.2 | async-start | bytes 49152 | tf_op jit(solution)/shard_map/all_to_all | solution.py:45
  495.0 9.7 %all-to-all-done.2 = f32[16,1,384]{2,1,0:T(1,128)S(1)} async-done(((f32[16,1,384]{2,1,0:T(1,128)}), f32[16,1,384]{2,1,0:T(1,128)S(1)}, u32[]{:S(2)}, u32[]{:S(2)}) %all-to-all-start.2) | async-done | bytes 24608 | tf_op jit(solution)/shard_map/all_to_all | solution.py:45
  504.8 0.5 add_subtract_fusion
  505.3 16.6 %reduce-scatter.5.cloned.1.call-done = f32[128,768]{0,1:T(8,128)} async-done(((f32[512,768]{0,1:T(8,128)}), f32[128,768]{0,1:T(8,128)}) %reduce-scatter.5.cloned.1.call-update) | async-done | bytes 393232 | tf_op jit(solution)/shard_map/reduce_scatter | solution.py:52
  521.9 1.1 bitcast_select_fusion
  522.9 0.9 copy.31
  (47 shorter events, 0.6 us)
Async XLA Ops:
  7.2 2.9 copy-start
  7.2 243.9 %all-gather.2.cloned.1.call-start = ((), (), s32[]{:S(2)}) async-start(), calls=%async_computation.5 | async-start | bytes 8355840 | tf_op jit(solution)/shard_map/all_gather | solution.py:35
  10.0 9.5 %copy-start.3 = (s32[2048]{0:T(1024)S(1)}, s32[2048]{0:T(1024)}, u32[]{:S(2)}) copy-start(s32[2048]{0:T(1024)} %param.10) | copy-start | bytes 24580
  182.0 69.1 %copy-start.1 = (bf16[128,768]{1,0:T(8,128)(2,1)}, bf16[128,768]{1,0:T(8,128)(2,1)S(1)}, u32[]{:S(2)}) copy-start(bf16[128,768]{1,0:T(8,128)(2,1)S(1)} %reduce_sum.84) | copy-start | bytes 589828
  257.3 5.0 copy-start.4
  257.3 5.0 copy-start.5
  264.4 9.9 %copy-start.2 = (s32[32768]{0:T(1024)S(1)}, s32[32768]{0:T(1024)}, u32[]{:S(2)}) copy-start(s32[32768]{0:T(1024)} %param.17) | copy-start | bytes 393220
  264.4 52.3 %all-to-all-start.1 = ((bf16[16,128,768]{2,1,0:T(8,128)(2,1)}), bf16[16,128,768]{2,1,0:T(8,128)(2,1)}, u32[]{:S(2)}, u32[]{:S(2)}) async-start(bf16[16,128,768]{2,1,0:T(8,128)(2,1)} %stack.2), calls=%async_computation.1 | async-start | bytes 6291456 | tf_op jit(solution)/shard_map/all_to_all | solution.py:18
  274.3 204.3 %reduce-scatter.3.cloned.1.call-start = ((), (), s32[]{:S(2)}) async-start(), calls=%async_computation.6 | async-start | bytes 7864320 | tf_op jit(solution)/shard_map/reduce_scatter | solution.py:52
  374.6 147.3 %reduce-scatter.5.cloned.1.call-start = ((), (), s32[]{:S(2)}) async-start(), calls=%async_computation.7 | async-start | bytes 1966080 | tf_op jit(solution)/shard_map/reduce_scatter | solution.py:52
  485.0 19.8 %all-to-all-start.2 = ((f32[16,1,384]{2,1,0:T(1,128)}), f32[16,1,384]{2,1,0:T(1,128)S(1)}, u32[]{:S(2)}, u32[]{:S(2)}) async-start(f32[16,1,384]{2,1,0:T(1,128)} %all_to_all.16), calls=%async_computation.2 | async-start | bytes 49152 | tf_op jit(solution)/shard_map/all_to_all | solution.py:45
Sparse Core Ops, SparseCore 0:
  9.8 241.2 all-gather.1
  374.7 103.8 reduce-scatter.2
  481.2 40.6 reduce-scatter.4
